TPU v7x, 1024 devices: a whole 4x4x32 slice. The times are simulated.
1024 devices in a mesh: ctx: 64 (over x_hi, z), ch: 16 (over y, x_lo, core).
Axes of the slice: x: 4 (x_hi: 2, x_lo: 2; x = x_hi * 2 + x_lo), y: 4, z: 32, core: 2. Of those that a mesh axis runs over, the one named last changes fastest.
Arguments:
- inputs: bfloat16 [1536, 131072], P('ch', 'ctx'), may hold values from -6 to 6
- conv_weight: bfloat16 [3, 1536, 96], replicated, may hold values from -0.375 to 0.375
- pw_weight: bfloat16 [1536, 1536], replicated, may hold values from -0.15625 to 0.15625
- cotangent: bfloat16 [1536, 131072], P(None, ('ctx', 'ch')), may hold values from -6 to 6
Outputs:
- mixed: bfloat16 [1536, 131072], P(None, ('ctx', 'ch'))
- grad_inputs: bfloat16 [1536, 131072], P('ch', 'ctx')
All inputs are finite; a program needn't handle non-finite values.
Results may differ from a plain program's by a relative error of at most 0.012.
Values may be sent and summed in bfloat16 or wider, within the bound.
A program may use at most 32 MiB of HBM per device.

v0:
```python
import jax
import jax.numpy as jnp
from jax import lax
from jax.sharding import PartitionSpec as P

DILATION_STEP = 512


def shifted(block, axis, distance):
    devices = range(lax.axis_size(axis))
    route = [(i - distance, i) for i in devices if i - distance in devices]
    return lax.ppermute(block, axis, route)


def gelu_slope(values):
    return jax.vjp(jax.nn.gelu, values)[1](jnp.ones_like(values))[0]


def group_conv(kernel_taps, weight_part):
    channels, length = kernel_taps[0].shape
    width = weight_part.shape[2]
    groups = channels // width
    total = jnp.zeros((groups, width, length), jnp.float32)
    for position_offset in range(3):
        kernel = weight_part[position_offset].reshape(groups, width, width)
        signal = kernel_taps[position_offset].reshape(groups, width, length)
        total = total + jnp.einsum(
            "gji,gip->gjp", kernel, signal, preferred_element_type=jnp.float32
        )
    return total.reshape(channels, length)


def group_conv_back(kernel_taps, weight_part):
    channels, length = kernel_taps[0].shape
    width = weight_part.shape[2]
    groups = channels // width
    total = jnp.zeros((groups, width, length), jnp.float32)
    for position_offset in range(3):
        kernel = weight_part[position_offset].reshape(groups, width, width)
        signal = kernel_taps[position_offset].reshape(groups, width, length)
        total = total + jnp.einsum(
            "gji,gjp->gip", kernel, signal, preferred_element_type=jnp.float32
        )
    return total.reshape(channels, length)


def upstream_grad(pw_weight, cotangent):
    return lax.dot_general(
        pw_weight, cotangent, (((0,), (0,)), ((), ())), preferred_element_type=jnp.float32
    ).astype(jnp.bfloat16)


def shift_rows(values, steps):
    return shifted(values, ("ctx", "ch"), steps)


def shift_grads(values, steps):
    return shifted(values, ("ctx", "ch"), steps)


def body(inputs, conv_weight, pw_weight, cotangent):
    track_rows = lax.all_to_all(inputs, "ch", split_axis=1, concat_axis=0, tiled=True)
    position_stride = DILATION_STEP // track_rows.shape[1]
    kernel_taps = [
        shift_rows(track_rows, position_stride),
        track_rows,
        shift_rows(track_rows, -position_stride),
    ]
    conv_out = group_conv(kernel_taps, conv_weight)
    active = jax.nn.gelu(conv_out).astype(jnp.bfloat16)
    mixed = jnp.dot(pw_weight, active, preferred_element_type=jnp.float32).astype(jnp.bfloat16)
    grad_active = upstream_grad(pw_weight, cotangent)
    convolved_gradient = (grad_active.astype(jnp.float32) * gelu_slope(conv_out)).astype(
        jnp.bfloat16
    )
    back_taps = [
        shift_grads(convolved_gradient, -position_stride),
        convolved_gradient,
        shift_grads(convolved_gradient, position_stride),
    ]
    grad_rows = group_conv_back(back_taps, conv_weight).astype(jnp.bfloat16)
    grad_inputs = lax.all_to_all(grad_rows, "ch", split_axis=0, concat_axis=1, tiled=True)
    return (mixed, grad_inputs)


def solution(mesh):
    placed = (P("ch", "ctx"), P(), P(), P(None, ("ctx", "ch")))
    return jax.shard_map(
        body,
        mesh=mesh,
        in_specs=placed,
        out_specs=(P(None, ("ctx", "ch")), P("ch", "ctx")),
        check_vma=False,
    )
```

profile of v0, /device:TPU:4, one launch (start us, length us, event | category | flops | bytes accessed | tf_op | source)
XLA Modules:
  0.0 90.8 jit_solution(12302581422439729503)
XLA Ops:
  0.6 0.0 copy-start
  0.6 1.0 %copy-done = bf16[96,2048]{1,0:T(8,128)(2,1)S(1)} copy-done((bf16[96,2048]{1,0:T(8,128)(2,1)S(1)}, bf16[96,2048]{1,0:T(8,128)(2,1)}, u32[]{:S(2)}) %copy-start) | copy-done | bytes 393240
  1.6 0.1 copy_bitcast_fusion.1
  1.7 14.5 %all_to_all.35 = bf16[96,16,128]{2,0,1:T(8,128)(2,1)S(1)} all-to-all(bf16[96,16,128]{2,0,1:T(8,128)(2,1)S(1)} %copy_bitcast_fusion.1), channel_id=1, replica_groups=mesh['ctx'=64,'ch'=16] {'ch'}, dimensions={1} | all-to-all | bytes 786432 | tf_op jit(solution)/shard_map/all_to_all | solution.py:62
  16.2 19.2 %collective-permute-start.1 = (bf16[1536,128]{1,0:T(8,128)(2,1)S(1)}, bf16[1536,128]{1,0:T(8,128)(2,1)S(1)}, u32[]{:S(2)}, u32[]{:S(2)}) collective-permute-start(bf16[1536,128]{1,0:T(8,128)(2,1)S(1)} %bitcast.63), channel_id=1, source_target_pairs={{4,0},{5,1},{6,2},{7,3},{8,4},{9,5},{10,6},{11,7},{12,8},{13,9},{1... | collective-permute-start | bytes 1179656 | tf_op jit(solution)/shard_map/ppermute | solution.py:12
  35.4 1.2 %fusion.18 = (bf16[1,1536,96]{1,2,0:T(8,128)(2,1)S(1)}, bf16[1,1536,96]{1,2,0:T(8,128)(2,1)S(1)}, bf16[1,1536,96]{1,2,0:T(8,128)(2,1)S(1)}) fusion(bf16[3,1536,96]{1,2,0:T(8,128)(2,1)} %param.5), kind=kLoop, calls=%fused_computation.28 | loop fusion | bytes 1769472 | tf_op jit(solution)/shard_map/slice | solution.py:25
  36.6 0.2 copy.13
  36.8 0.2 copy.16
  37.0 0.0 copy-start.2
  37.0 0.2 copy.15
  37.3 0.0 copy-start.1
  37.3 2.2 %collective-permute-start = (bf16[1536,128]{1,0:T(8,128)(2,1)S(1)}, bf16[1536,128]{1,0:T(8,128)(2,1)S(1)}, u32[]{:S(2)}, u32[]{:S(2)}) collective-permute-start(bf16[1536,128]{1,0:T(8,128)(2,1)S(1)} %bitcast.64), channel_id=1, source_target_pairs={{0,4},{1,5},{2,6},{3,7},{4,8},{5,9},{6,10},{7,11},{8,12},{9,13},{1... | collective-permute-start | bytes 1179656 | tf_op jit(solution)/shard_map/ppermute | solution.py:12
  39.5 0.2 fusion.16
  39.7 3.5 %collective-permute-done.1 = bf16[1536,128]{1,0:T(8,128)(2,1)S(1)} collective-permute-done((bf16[1536,128]{1,0:T(8,128)(2,1)S(1)}, bf16[1536,128]{1,0:T(8,128)(2,1)S(1)}, u32[]{:S(2)}, u32[]{:S(2)}) %collective-permute-start.1) | collective-permute-done | bytes 393248 | tf_op jit(solution)/shard_map/ppermute | solution.py:12
  43.2 0.2 fusion.19
  43.5 11.8 %collective-permute-done = bf16[1536,128]{1,0:T(8,128)(2,1)S(1)} collective-permute-done((bf16[1536,128]{1,0:T(8,128)(2,1)S(1)}, bf16[1536,128]{1,0:T(8,128)(2,1)S(1)}, u32[]{:S(2)}, u32[]{:S(2)}) %collective-permute-start) | collective-permute-done | bytes 393248 | tf_op jit(solution)/shard_map/ppermute | solution.py:12
  55.3 0.3 fusion.4
  55.5 0.4 fusion.11
  55.9 0.0 copy-done.2
  55.9 1.5 %fusion.2 = bf16[1536,128]{1,0:T(8,128)(2,1)S(1)} fusion(bf16[1536,1536]{1,0:T(8,128)(2,1)S(1)} %copy-done.1, bf16[1536,128]{1,0:T(8,128)(2,1)S(1)} %copy-done.2, f32[1536,128]{1,0:T(8,128)S(1)} %bitcast.55, f32[1536,128]{1,0:T(8,128)S(1)} %get-tuple-element.10, f32[1536,128]{1,0:T(8,128)S(1)} %get-tuple-element.9), kind=kOutput, calls=%fused_computation.4 | convolution fusion | flops 606535680 | bytes 7864320 | tf_op jit(solution)/shard_map/dot_general | solution.py:48
  57.4 1.9 %collective-permute-start.3 = (bf16[1536,128]{1,0:T(8,128)(2,1)S(1)}, bf16[1536,128]{1,0:T(8,128)(2,1)S(1)}, u32[]{:S(2)}, u32[]{:S(2)}) collective-permute-start(bf16[1536,128]{1,0:T(8,128)(2,1)S(1)} %fusion.2), channel_id=1, source_target_pairs={{0,4},{1,5},{2,6},{3,7},{4,8},{5,9},{6,10},{7,11},{8,12},{9,13},{1... | collective-permute-start | bytes 1179656 | tf_op jit(solution)/shard_map/ppermute | solution.py:12
  59.3 9.6 %collective-permute-start.2 = (bf16[1536,128]{1,0:T(8,128)(2,1)S(1)}, bf16[1536,128]{1,0:T(8,128)(2,1)S(1)}, u32[]{:S(2)}, u32[]{:S(2)}) collective-permute-start(bf16[1536,128]{1,0:T(8,128)(2,1)S(1)} %fusion.2), channel_id=1, source_target_pairs={{4,0},{5,1},{6,2},{7,3},{8,4},{9,5},{10,6},{11,7},{12,8},{13,9},{1... | collective-permute-start | bytes 1179656 | tf_op jit(solution)/shard_map/ppermute | solution.py:12
  69.0 0.3 fusion.20
  69.3 4.9 %collective-permute-done.3 = bf16[1536,128]{1,0:T(8,128)(2,1)S(1)} collective-permute-done((bf16[1536,128]{1,0:T(8,128)(2,1)S(1)}, bf16[1536,128]{1,0:T(8,128)(2,1)S(1)}, u32[]{:S(2)}, u32[]{:S(2)}) %collective-permute-start.3) | collective-permute-done | bytes 393248 | tf_op jit(solution)/shard_map/ppermute | solution.py:12
  74.2 0.3 fusion.21
  74.5 0.9 %collective-permute-done.2 = bf16[1536,128]{1,0:T(8,128)(2,1)S(1)} collective-permute-done((bf16[1536,128]{1,0:T(8,128)(2,1)S(1)}, bf16[1536,128]{1,0:T(8,128)(2,1)S(1)}, u32[]{:S(2)}, u32[]{:S(2)}) %collective-permute-start.2) | collective-permute-done | bytes 393248 | tf_op jit(solution)/shard_map/ppermute | solution.py:12
  75.4 1.1 %fusion.7 = bf16[16,96,128]{2,1,0:T(8,128)(2,1)} fusion(f32[16,128,96]{1,2,0:T(8,128)S(1)} %fusion.21, f32[16,128,96]{1,2,0:T(8,128)S(1)} %fusion.20, bf16[16,96,128]{2,1,0:T(8,128)(2,1)S(1)} %bitcast.68, bf16[16,96,96]{2,1,0:T(8,128)(2,1)S(1)} %bitcast.57), kind=kOutput, calls=%fused_computation.11 | convolution fusion | flops 38338560 | bytes 2654208 | tf_op jit(solution)/shard_map/gji,gjp->gip/dot_general | solution.py:41
  76.4 4.1 %all-to-all-start.1 = ((bf16[16,96,128]{2,1,0:T(8,128)(2,1)}), bf16[16,96,128]{2,1,0:T(8,128)(2,1)S(1)}, u32[]{:S(2)}, u32[]{:S(2)}) async-start(bf16[16,96,128]{2,1,0:T(8,128)(2,1)} %fusion.7), calls=%async_computation.1 | async-start | bytes 786432 | tf_op jit(solution)/shard_map/all_to_all | solution.py:82
  80.6 4.0 %fusion.3 = bf16[1536,128]{0,1:T(8,128)(2,1)S(1)} fusion(bf16[1536,128]{1,0:T(8,128)(2,1)S(1)} %get-tuple-element.11, bf16[1536,1536]{1,0:T(8,128)(2,1)} %param.6), kind=kOutput, calls=%fused_computation.5 | convolution fusion | flops 604176384 | bytes 5505024 | tf_op jit(solution)/shard_map/dot_general | solution.py:71
  84.6 0.9 %copy.21 = bf16[1536,128]{1,0:T(8,128)(2,1)} copy(bf16[1536,128]{0,1:T(8,128)(2,1)S(1)} %fusion.3) | data formatting | bytes 786432
  85.5 4.5 %all-to-all-done.1 = bf16[16,96,128]{2,1,0:T(8,128)(2,1)S(1)} async-done(((bf16[16,96,128]{2,1,0:T(8,128)(2,1)}), bf16[16,96,128]{2,1,0:T(8,128)(2,1)S(1)}, u32[]{:S(2)}, u32[]{:S(2)}) %all-to-all-start.1) | async-done | bytes 393248 | tf_op jit(solution)/shard_map/all_to_all | solution.py:82
  90.0 0.8 copy_bitcast_fusion
  (1 shorter events, 0.0 us)
Async XLA Ops:
  0.6 1.0 %copy-start = (bf16[96,2048]{1,0:T(8,128)(2,1)S(1)}, bf16[96,2048]{1,0:T(8,128)(2,1)}, u32[]{:S(2)}) copy-start(bf16[96,2048]{1,0:T(8,128)(2,1)} %param.4) | copy-start | bytes 1179652
  16.2 27.1 %collective-permute-start.1 = (bf16[1536,128]{1,0:T(8,128)(2,1)S(1)}, bf16[1536,128]{1,0:T(8,128)(2,1)S(1)}, u32[]{:S(2)}, u32[]{:S(2)}) collective-permute-start(bf16[1536,128]{1,0:T(8,128)(2,1)S(1)} %bitcast.63), channel_id=1, source_target_pairs={{4,0},{5,1},{6,2},{7,3},{8,4},{9,5},{10,6},{11,7},{12,8},{13,9},{1... | collective-permute-start | bytes 1179656 | tf_op jit(solution)/shard_map/ppermute | solution.py:12
  37.0 18.8 %copy-start.2 = (bf16[1536,128]{1,0:T(8,128)(2,1)S(1)}, bf16[1536,128]{1,0:T(8,128)(2,1)}, u32[]{:S(2)}) copy-start(bf16[1536,128]{1,0:T(8,128)(2,1)} %param.7) | copy-start | bytes 1179652
  37.3 18.6 %copy-start.1 = (bf16[1536,1536]{1,0:T(8,128)(2,1)S(1)}, bf16[1536,1536]{1,0:T(8,128)(2,1)}, u32[]{:S(2)}) copy-start(bf16[1536,1536]{1,0:T(8,128)(2,1)} %param.6) | copy-start | bytes 14155780
  37.3 18.0 %collective-permute-start = (bf16[1536,128]{1,0:T(8,128)(2,1)S(1)}, bf16[1536,128]{1,0:T(8,128)(2,1)S(1)}, u32[]{:S(2)}, u32[]{:S(2)}) collective-permute-start(bf16[1536,128]{1,0:T(8,128)(2,1)S(1)} %bitcast.64), channel_id=1, source_target_pairs={{0,4},{1,5},{2,6},{3,7},{4,8},{5,9},{6,10},{7,11},{8,12},{9,13},{1... | collective-permute-start | bytes 1179656 | tf_op jit(solution)/shard_map/ppermute | solution.py:12
  57.4 16.8 %collective-permute-start.3 = (bf16[1536,128]{1,0:T(8,128)(2,1)S(1)}, bf16[1536,128]{1,0:T(8,128)(2,1)S(1)}, u32[]{:S(2)}, u32[]{:S(2)}) collective-permute-start(bf16[1536,128]{1,0:T(8,128)(2,1)S(1)} %fusion.2), channel_id=1, source_target_pairs={{0,4},{1,5},{2,6},{3,7},{4,8},{5,9},{6,10},{7,11},{8,12},{9,13},{1... | collective-permute-start | bytes 1179656 | tf_op jit(solution)/shard_map/ppermute | solution.py:12
  59.3 16.1 %collective-permute-start.2 = (bf16[1536,128]{1,0:T(8,128)(2,1)S(1)}, bf16[1536,128]{1,0:T(8,128)(2,1)S(1)}, u32[]{:S(2)}, u32[]{:S(2)}) collective-permute-start(bf16[1536,128]{1,0:T(8,128)(2,1)S(1)} %fusion.2), channel_id=1, source_target_pairs={{4,0},{5,1},{6,2},{7,3},{8,4},{9,5},{10,6},{11,7},{12,8},{13,9},{1... | collective-permute-start | bytes 1179656 | tf_op jit(solution)/shard_map/ppermute | solution.py:12
  76.4 13.6 %all-to-all-start.1 = ((bf16[16,96,128]{2,1,0:T(8,128)(2,1)}), bf16[16,96,128]{2,1,0:T(8,128)(2,1)S(1)}, u32[]{:S(2)}, u32[]{:S(2)}) async-start(bf16[16,96,128]{2,1,0:T(8,128)(2,1)} %fusion.7), calls=%async_computation.1 | async-start | bytes 786432 | tf_op jit(solution)/shard_map/all_to_all | solution.py:82
where the time goes:
time: 91.2 us; the launch traced here: 90.8 us
  starting transfers between devices  37.1 us (41%)
  waiting for transfers between devices  25.6 us (28%)
  blocking collectives  14.5 us (16%)
  matrix products  7.88 us (9%)
  local copies, waits for them, and re-layouts  4.65 us (5%)
    ppermute x4, starting transfers between devices, shifted(): return lax.ppermute(block, axis, route)  32.9 us
    ppermute x4, waiting for transfers between devices, shifted(): return lax.ppermute(block, axis, route)  21.1 us
    all_to_all x1, blocking collectives, body(): lax.all_to_all(inputs, 'ch', split_axis=1, concat_axis=0, tiled=True)  14.5 us
    all_to_all x1, waiting for transfers between devices, body(): lax.all_to_all(grad_rows, 'ch', split_axis=0, concat_axis=1, tiled=True)  4.53 us
    all_to_all x1, starting transfers between devices, body(): lax.all_to_all(grad_rows, 'ch', split_axis=0, concat_axis=1, tiled=True)  4.12 us
    dot_general x1, matrix products, body(): jnp.dot(pw_weight, active, preferred_element_type=jnp.float32)  4 us
    unnamed x7, local copies, waits for them, and re-layouts  1.93 us
    slice x4, local copies, waits for them, and re-layouts, group_conv(): kernel = weight_part[position_offset].reshape(groups, width, width)  1.87 us
  transfers between devices with their start and end apart: 5, of which 5 were waited for; matrix products, arithmetic and copies ran while one was open for 9% of the time, Pallas kernels for 0%

commit v1 on v0

v1 whole, which is shorter than its diff:
```python
import functools

import jax
import jax.numpy as jnp
from jax import lax
from jax.experimental import pallas as pl
from jax.experimental.pallas import tpu as pltpu
from jax.sharding import PartitionSpec as P

STEP = 512
TAPS = 3
CUBIC = 0.044715
SCALE = 0.7978845608028654
NT = (((1,), (1,)), ((), ()))


def gelu_and_slope(v):
    square = v * v
    t = jnp.tanh(SCALE * v * (1.0 + CUBIC * square))
    half = 0.5 * (1.0 + t)
    slope = half + 0.5 * v * (1.0 - t * t) * (SCALE * (1.0 + 3.0 * CUBIC * square))
    return v * half, slope


def kernel(
    n_ctx, x_hbm, wt_hbm, pw_hbm, cot_hbm, mixed_ref, gin_ref,
    xc, gc, wwin, pw_v, cot_v, cot_t, slope, act_send, act_recv, ga_send, ga_recv, total,
    load_sem, halo_send, halo_recv, act_ssem, act_rsem, ga_ssem, ga_rsem,
):
    width, block = act_send.shape[1:]
    quads = 4
    me_ctx, me = lax.axis_index("ctx"), lax.axis_index("ch")
    y, x, core = me // 4, (me // 2) % 2, me % 2
    wide = quads * width

    barrier = pltpu.get_barrier_semaphore()
    for k in range(1, 16):
        pl.semaphore_signal(barrier, inc=1, device_id={"ch": lax.rem(me + k, 16)})

    @pl.when(me_ctx > 0)
    def _():
        pl.semaphore_signal(barrier, inc=1, device_id={"ctx": me_ctx - 1})

    @pl.when(me_ctx < n_ctx - 1)
    def _():
        pl.semaphore_signal(barrier, inc=1, device_id={"ctx": me_ctx + 1})

    start = jnp.minimum((width * me) // 128, (16 * width) // 128 - 2) * 128
    off = width * me - start
    w_load = pltpu.make_async_copy(
        wt_hbm.at[:, :, pl.ds(pl.multiple_of(start, 128), 256)], wwin, load_sem.at[0]
    )
    w_load.start()
    x_loads = []
    for q in range(4):
        x_loads.append(
            pltpu.make_async_copy(x_hbm.at[:, pl.ds(STEP * q, STEP)], xc.at[q + 1], load_sem.at[1 + q])
        )
        x_loads[-1].start()
    cot_load = pltpu.make_async_copy(cot_hbm, cot_v, load_sem.at[5])
    cot_load.start()
    order = (1, 3, 2, 0)
    pw_loads = []
    for n, dy in enumerate(order):
        at = pl.multiple_of(lax.rem(y + dy, 4) * wide, 128)
        pw_loads.append(
            pltpu.make_async_copy(pw_hbm.at[:, pl.ds(at, wide)], pw_v.at[n], load_sem.at[6 + n])
        )
        pw_loads[-1].start()

    w_load.wait()
    rows = lax.broadcasted_iota(jnp.int32, (width, 256), 0)
    lanes = lax.broadcasted_iota(jnp.int32, (width, 256), 1)
    pick = jnp.where(lanes == rows + off, 1.0, 0.0).astype(jnp.bfloat16)
    w_cat = lax.dot_general(
        pick, wwin[...].reshape(TAPS * width, 256), NT, preferred_element_type=jnp.float32
    ).astype(jnp.bfloat16)
    depth = lax.broadcasted_iota(jnp.int32, (256, TAPS * width), 0)
    column = lax.broadcasted_iota(jnp.int32, (256, TAPS * width), 1)
    wt_cat = jnp.zeros((width, TAPS * width), jnp.float32)
    for t in range(TAPS):
        hit = (depth == column - width * t + off) & (column >= width * t) & (column < width * (t + 1))
        place = jnp.where(hit, 1.0, 0.0).astype(jnp.bfloat16)
        wt_cat = wt_cat + jnp.dot(wwin[t], place, preferred_element_type=jnp.float32)
    wt_cat = wt_cat.astype(jnp.bfloat16)

    def conv(q):
        signal = jnp.concatenate([xc[q], xc[q + 1], xc[q + 2]], axis=0)
        act, tilt = gelu_and_slope(jnp.dot(w_cat, signal, preferred_element_type=jnp.float32))
        slope[q] = tilt
        act = act.astype(jnp.bfloat16)
        for b in range(4):
            act_send[4 * q + b] = act[:, block * b : block * (b + 1)]

    def send_act(q):
        for n, (dx, dc) in enumerate(((1, 0), (1, 1), (0, 1), (0, 0))):
            to = 4 * q + 2 * lax.rem(x + dx, 2) + lax.rem(core + dc, 2)
            copy = pltpu.make_async_remote_copy(
                src_ref=act_send.at[to],
                dst_ref=act_recv.at[pl.ds(pl.multiple_of(width * me, width), width), :],
                send_sem=act_ssem.at[4 * q + n],
                recv_sem=act_rsem.at[me],
                device_id={"ch": to},
            )
            if dx or dc:
                copy.start()
            else:
                pl.when(y != q)(copy.start)

                @pl.when(y == q)
                def _():
                    pltpu.make_async_copy(
                        act_send.at[to],
                        act_recv.at[pl.ds(pl.multiple_of(width * me, width), width), :],
                        act_rsem.at[me],
                    ).start()

    def wait_sent(q_sems, buffer):
        pltpu.make_async_copy(buffer, buffer, q_sems).wait()

    for q in range(4):
        x_loads[q].wait()
    conv(1)
    conv(2)

    pl.semaphore_wait(barrier, 15 + (me_ctx > 0).astype(jnp.int32) + (me_ctx < n_ctx - 1).astype(jnp.int32))

    def halo(buffer, side, base):
        return pltpu.make_async_remote_copy(
            src_ref=buffer.at[1 if side == 0 else 4],
            dst_ref=buffer.at[5 if side == 0 else 0],
            send_sem=halo_send.at[base + side],
            recv_sem=halo_recv.at[base + side],
            device_id={"ctx": me_ctx - 1 if side == 0 else me_ctx + 1},
        )

    has_left, has_right = me_ctx > 0, me_ctx < n_ctx - 1
    pl.when(has_left)(lambda: halo(xc, 0, 0).start())
    pl.when(has_right)(lambda: halo(xc, 1, 0).start())
    send_act(1)
    send_act(2)

    cot_load.wait()
    cot_t[...] = cot_v[...].T
    for n, dy in enumerate(order):
        pw_loads[n].wait()
        part = jnp.dot(cot_t[...], pw_v[n], preferred_element_type=jnp.float32)
        to_y = lax.rem(y + dy, 4)
        flipped = part.T.astype(jnp.bfloat16)
        for b in range(4):
            ga_send[4 * n + b] = flipped[width * b : width * (b + 1), :]
        for k, (dx, dc) in enumerate(((1, 0), (1, 1), (0, 1), (0, 0))):
            low = 2 * lax.rem(x + dx, 2) + lax.rem(core + dc, 2)
            if dy or dx or dc:
                pltpu.make_async_remote_copy(
                    src_ref=ga_send.at[4 * n + low],
                    dst_ref=ga_recv.at[me],
                    send_sem=ga_ssem.at[4 * n + k],
                    recv_sem=ga_rsem.at[me],
                    device_id={"ch": 4 * to_y + low},
                ).start()
            else:
                pltpu.make_async_copy(ga_send.at[4 * n + low], ga_recv.at[me], ga_rsem.at[me]).start()

    @pl.when(has_left)
    def _():
        halo(xc, 1, 0).wait_recv()

    @pl.when(jnp.logical_not(has_left))
    def _():
        xc[0] = jnp.zeros(xc.shape[1:], xc.dtype)

    conv(0)
    send_act(0)

    @pl.when(has_right)
    def _():
        halo(xc, 0, 0).wait_recv()

    @pl.when(jnp.logical_not(has_right))
    def _():
        xc[5] = jnp.zeros(xc.shape[1:], xc.dtype)

    conv(3)
    send_act(3)

    def grad_conv(q):
        for b in range(4):
            s = 4 * q + b
            pltpu.make_async_copy(ga_recv.at[s], ga_recv.at[s], ga_rsem.at[s]).wait()
            gc[q + 1, :, pl.ds(block * b, block)] = (
                ga_recv[s].astype(jnp.float32) * slope[q, :, pl.ds(block * b, block)]
            ).astype(jnp.bfloat16)

    grad_conv(0)
    pl.when(has_left)(lambda: halo(gc, 0, 2).start())
    grad_conv(3)
    pl.when(has_right)(lambda: halo(gc, 1, 2).start())
    grad_conv(1)
    grad_conv(2)

    def back(q):
        signal = jnp.concatenate([gc[q + 2], gc[q + 1], gc[q]], axis=0)
        gin_ref[:, pl.ds(STEP * q, STEP)] = jnp.dot(
            wt_cat, signal, preferred_element_type=jnp.float32
        ).astype(jnp.bfloat16)

    back(1)
    back(2)

    @pl.when(has_left)
    def _():
        halo(gc, 1, 2).wait_recv()

    @pl.when(jnp.logical_not(has_left))
    def _():
        gc[0] = jnp.zeros(gc.shape[1:], gc.dtype)

    back(0)

    @pl.when(has_right)
    def _():
        halo(gc, 0, 2).wait_recv()

    @pl.when(jnp.logical_not(has_right))
    def _():
        gc[5] = jnp.zeros(gc.shape[1:], gc.dtype)

    back(3)

    visit = (3, 0, 1, 2)
    for k, n in enumerate(visit):
        from_y = lax.rem(y + order[n], 4)
        for b in range(4):
            s = 4 * from_y + b
            piece = act_recv.at[pl.ds(pl.multiple_of(width * s, width), width), :]
            pltpu.make_async_copy(piece, piece, act_rsem.at[s]).wait()
        part = jnp.dot(
            pw_v[n],
            act_recv[pl.ds(pl.multiple_of(wide * from_y, wide), wide), :],
            preferred_element_type=jnp.float32,
        )
        if k == 0:
            total[...] = part
        elif k < 3:
            total[...] += part
        else:
            mixed_ref[...] = (total[...] + part).astype(jnp.bfloat16)

    for q in range(4):
        for n in range(4):
            if n < 3:
                wait_sent(act_ssem.at[4 * q + n], act_send.at[0])
            else:
                pl.when(y != q)(lambda: wait_sent(act_ssem.at[4 * q + n], act_send.at[0]))
            if order[q] or n < 3:
                wait_sent(ga_ssem.at[4 * q + n], ga_send.at[0])
    for base, buffer in ((0, xc), (2, gc)):
        pl.when(has_left)(lambda: halo(buffer, 0, base).wait_send())
        pl.when(has_right)(lambda: halo(buffer, 1, base).wait_send())


def body(n_ctx, inputs, conv_weight, pw_weight, cotangent):
    width, length = inputs.shape
    channels, block = cotangent.shape
    bf16, f32 = jnp.bfloat16, jnp.float32
    dma = pltpu.SemaphoreType.DMA
    return pl.pallas_call(
        functools.partial(kernel, n_ctx),
        out_shape=(
            jax.ShapeDtypeStruct((channels, block), bf16),
            jax.ShapeDtypeStruct((width, length), bf16),
        ),
        in_specs=[pl.BlockSpec(memory_space=pl.ANY)] * 4,
        out_specs=[pl.BlockSpec(memory_space=pltpu.VMEM)] * 2,
        scratch_shapes=[
            pltpu.VMEM((6, width, STEP), bf16),
            pltpu.VMEM((6, width, STEP), bf16),
            pltpu.VMEM((TAPS, width, 256), bf16),
            pltpu.VMEM((4, channels, 4 * width), bf16),
            pltpu.VMEM((channels, block), bf16),
            pltpu.VMEM((block, channels), bf16),
            pltpu.VMEM((4, width, STEP), f32),
            pltpu.VMEM((16, width, block), bf16),
            pltpu.VMEM((channels, block), bf16),
            pltpu.VMEM((16, width, block), bf16),
            pltpu.VMEM((16, width, block), bf16),
            pltpu.VMEM((channels, block), f32),
            dma((10,)),
            dma((4,)),
            dma((4,)),
            dma((16,)),
            dma((16,)),
            dma((16,)),
            dma((16,)),
        ],
        compiler_params=pltpu.CompilerParams(
            collective_id=0, has_side_effects=True, vmem_limit_bytes=40 * 1024 * 1024
        ),
        name="conv_mix_grad",
    )(*(
        pltpu.with_memory_space_constraint(a, pltpu.HBM)
        for a in (inputs, jnp.transpose(conv_weight, (0, 2, 1)), pw_weight, cotangent)
    ))


def solution(mesh):
    return jax.shard_map(
        functools.partial(body, mesh.shape["ctx"]),
        mesh=mesh,
        in_specs=(P("ch", "ctx"), P(), P(), P(None, ("ctx", "ch"))),
        out_specs=(P(None, ("ctx", "ch")), P("ch", "ctx")),
        check_vma=False,
    )
```

time: 91.2 us -> 40.2 us (0.44)
  the two profiles are of different devices: /device:TPU:4 before, /device:TPU:20 now
where the time goes in v1:
time: 40.2 us; the launch traced here: 40.1 us
  Pallas kernels  37.9 us (94%)
  local copies, waits for them, and re-layouts  1.49 us (4%)
  between operations  0.64 us (2%)
    pallas_call x1, Pallas kernels, body(): pl.pallas_call(functools.partial(kernel, n_ctx), out_shape=(jax.ShapeDtyp...  37.9 us
    unnamed x2, local copies, waits for them, and re-layouts  1.49 us

profile of v1, /device:TPU:20, one launch (start us, length us, event | category | flops | bytes accessed | tf_op | source)
XLA Modules:
  0.0 40.1 jit_solution(6369767369306923363)
XLA Ops:
  0.6 37.9 %conv_mix_grad.1 = (bf16[1536,128]{1,0:T(8,128)(2,1)S(1)}, bf16[96,2048]{1,0:T(8,128)(2,1)S(1)}) custom-call(bf16[96,2048]{1,0:T(8,128)(2,1)} %x_hbm.1, bf16[3,96,1536]{2,1,0:T(8,128)(2,1)} %bitcast.1, bf16[1536,1536]{1,0:T(8,128)(2,1)} %pw_hbm.1, bf16[1536,128]{1,0:T(8,128)(2,1)} %cot_hbm.1), custom_call_target="tpu_custom_call" | custom-call | tf_op jit(solution)/shard_map/conv_mix_grad/pallas_call | solution.py:268
  38.6 0.7 %copy.8 = bf16[1536,128]{1,0:T(8,128)(2,1)} copy(bf16[1536,128]{1,0:T(8,128)(2,1)S(1)} %get-tuple-element.4) | data formatting | bytes 786432
  39.3 0.7 %copy.9 = bf16[96,2048]{1,0:T(8,128)(2,1)} copy(bf16[96,2048]{1,0:T(8,128)(2,1)S(1)} %get-tuple-element.5) | data formatting | bytes 786432

commit v2 on v1

--- a/solution.py
+++ b/solution.py
@@ -34,17 +34,32 @@
     wide = quads * width
 
     barrier = pltpu.get_barrier_semaphore()
+    has_left, has_right = me_ctx > 0, me_ctx < n_ctx - 1
+    seam = n_ctx // 2 - 1
     for k in range(1, 16):
         pl.semaphore_signal(barrier, inc=1, device_id={"ch": lax.rem(me + k, 16)})
 
-    @pl.when(me_ctx > 0)
+    @pl.when(has_left)
     def _():
         pl.semaphore_signal(barrier, inc=1, device_id={"ctx": me_ctx - 1})
 
-    @pl.when(me_ctx < n_ctx - 1)
+    @pl.when(has_right)
     def _():
         pl.semaphore_signal(barrier, inc=1, device_id={"ctx": me_ctx + 1})
 
+    cot_load = pltpu.make_async_copy(cot_hbm, cot_v, load_sem.at[5])
+    cot_load.start()
+    order = (1, 3, 2, 0)
+    pw_loads = []
+
+    def load_pw(n):
+        at = pl.multiple_of(lax.rem(y + order[n], 4) * wide, 128)
+        pw_loads.append(
+            pltpu.make_async_copy(pw_hbm.at[:, pl.ds(at, wide)], pw_v.at[n], load_sem.at[6 + n])
+        )
+        pw_loads[-1].start()
+
+    load_pw(0)
     start = jnp.minimum((width * me) // 128, (16 * width) // 128 - 2) * 128
     off = width * me - start
     w_load = pltpu.make_async_copy(
@@ -57,16 +72,52 @@
             pltpu.make_async_copy(x_hbm.at[:, pl.ds(STEP * q, STEP)], xc.at[q + 1], load_sem.at[1 + q])
         )
         x_loads[-1].start()
-    cot_load = pltpu.make_async_copy(cot_hbm, cot_v, load_sem.at[5])
-    cot_load.start()
-    order = (1, 3, 2, 0)
-    pw_loads = []
-    for n, dy in enumerate(order):
-        at = pl.multiple_of(lax.rem(y + dy, 4) * wide, 128)
-        pw_loads.append(
-            pltpu.make_async_copy(pw_hbm.at[:, pl.ds(at, wide)], pw_v.at[n], load_sem.at[6 + n])
+    for n in range(1, 4):
+        load_pw(n)
+
+    def halo(buffer, side, base):
+        return pltpu.make_async_remote_copy(
+            src_ref=buffer.at[1 if side == 0 else 4],
+            dst_ref=buffer.at[5 if side == 0 else 0],
+            send_sem=halo_send.at[base + side],
+            recv_sem=halo_recv.at[base + side],
+            device_id={"ctx": me_ctx - 1 if side == 0 else me_ctx + 1},
         )
-        pw_loads[-1].start()
+
+    cot_load.wait()
+    cot_t[...] = cot_v[...].T
+
+    def grad_active(n):
+        pw_loads[n].wait()
+        flipped = jnp.dot(cot_t[...], pw_v[n], preferred_element_type=jnp.float32).T.astype(jnp.bfloat16)
+        for b in range(4):
+            ga_send[4 * n + b] = flipped[width * b : width * (b + 1), :]
+
+    def send_ga(n):
+        dy = order[n]
+        for k, (dx, dc) in enumerate(((1, 0), (1, 1), (0, 1), (0, 0))):
+            low = 2 * lax.rem(x + dx, 2) + lax.rem(core + dc, 2)
+            if dy or dx or dc:
+                pltpu.make_async_remote_copy(
+                    src_ref=ga_send.at[4 * n + low],
+                    dst_ref=ga_recv.at[me],
+                    send_sem=ga_ssem.at[4 * n + k],
+                    recv_sem=ga_rsem.at[me],
+                    device_id={"ch": 4 * lax.rem(y + dy, 4) + low},
+                ).start()
+            else:
+                pltpu.make_async_copy(ga_send.at[4 * n + low], ga_recv.at[me], ga_rsem.at[me]).start()
+
+    grad_active(0)
+    for q in range(4):
+        x_loads[q].wait()
+    pl.semaphore_wait(barrier, 15 + has_left.astype(jnp.int32) + has_right.astype(jnp.int32))
+    pl.when(has_right)(lambda: halo(xc, 1, 0).start())
+    pl.when(has_left)(lambda: halo(xc, 0, 0).start())
+    send_ga(0)
+    for n in range(1, 4):
+        grad_active(n)
+        send_ga(n)
 
     w_load.wait()
     rows = lax.broadcasted_iota(jnp.int32, (width, 256), 0)
@@ -118,50 +169,11 @@
     def wait_sent(q_sems, buffer):
         pltpu.make_async_copy(buffer, buffer, q_sems).wait()
 
-    for q in range(4):
-        x_loads[q].wait()
     conv(1)
+    send_act(1)
     conv(2)
-
-    pl.semaphore_wait(barrier, 15 + (me_ctx > 0).astype(jnp.int32) + (me_ctx < n_ctx - 1).astype(jnp.int32))
-
-    def halo(buffer, side, base):
-        return pltpu.make_async_remote_copy(
-            src_ref=buffer.at[1 if side == 0 else 4],
-            dst_ref=buffer.at[5 if side == 0 else 0],
-            send_sem=halo_send.at[base + side],
-            recv_sem=halo_recv.at[base + side],
-            device_id={"ctx": me_ctx - 1 if side == 0 else me_ctx + 1},
-        )
-
-    has_left, has_right = me_ctx > 0, me_ctx < n_ctx - 1
-    pl.when(has_left)(lambda: halo(xc, 0, 0).start())
-    pl.when(has_right)(lambda: halo(xc, 1, 0).start())
-    send_act(1)
     send_act(2)
 
-    cot_load.wait()
-    cot_t[...] = cot_v[...].T
-    for n, dy in enumerate(order):
-        pw_loads[n].wait()
-        part = jnp.dot(cot_t[...], pw_v[n], preferred_element_type=jnp.float32)
-        to_y = lax.rem(y + dy, 4)
-        flipped = part.T.astype(jnp.bfloat16)
-        for b in range(4):
-            ga_send[4 * n + b] = flipped[width * b : width * (b + 1), :]
-        for k, (dx, dc) in enumerate(((1, 0), (1, 1), (0, 1), (0, 0))):
-            low = 2 * lax.rem(x + dx, 2) + lax.rem(core + dc, 2)
-            if dy or dx or dc:
-                pltpu.make_async_remote_copy(
-                    src_ref=ga_send.at[4 * n + low],
-                    dst_ref=ga_recv.at[me],
-                    send_sem=ga_ssem.at[4 * n + k],
-                    recv_sem=ga_rsem.at[me],
-                    device_id={"ch": 4 * to_y + low},
-                ).start()
-            else:
-                pltpu.make_async_copy(ga_send.at[4 * n + low], ga_recv.at[me], ga_rsem.at[me]).start()
-
     @pl.when(has_left)
     def _():
         halo(xc, 1, 0).wait_recv()
@@ -171,7 +183,7 @@
         xc[0] = jnp.zeros(xc.shape[1:], xc.dtype)
 
     conv(0)
-    send_act(0)
+    pl.when(me_ctx != seam)(lambda: send_act(0))
 
     @pl.when(has_right)
     def _():
@@ -182,7 +194,7 @@
         xc[5] = jnp.zeros(xc.shape[1:], xc.dtype)
 
     conv(3)
-    send_act(3)
+    pl.when(me_ctx != seam)(lambda: send_act(3))
 
     def grad_conv(q):
         for b in range(4):
@@ -192,10 +204,16 @@
                 ga_recv[s].astype(jnp.float32) * slope[q, :, pl.ds(block * b, block)]
             ).astype(jnp.bfloat16)
 
+    grad_conv(3)
+    pl.when(has_right)(lambda: halo(gc, 1, 2).start())
     grad_conv(0)
     pl.when(has_left)(lambda: halo(gc, 0, 2).start())
-    grad_conv(3)
-    pl.when(has_right)(lambda: halo(gc, 1, 2).start())
+
+    @pl.when(me_ctx == seam)
+    def _():
+        send_act(0)
+        send_act(3)
+
     grad_conv(1)
     grad_conv(2)
 
@@ -208,28 +226,10 @@
     back(1)
     back(2)
 
-    @pl.when(has_left)
-    def _():
-        halo(gc, 1, 2).wait_recv()
-
-    @pl.when(jnp.logical_not(has_left))
-    def _():
-        gc[0] = jnp.zeros(gc.shape[1:], gc.dtype)
-
-    back(0)
-
-    @pl.when(has_right)
-    def _():
-        halo(gc, 0, 2).wait_recv()
-
-    @pl.when(jnp.logical_not(has_right))
-    def _():
-        gc[5] = jnp.zeros(gc.shape[1:], gc.dtype)
-
-    back(3)
-
     visit = (3, 0, 1, 2)
-    for k, n in enumerate(visit):
+
+    def mix(k):
+        n = visit[k]
         from_y = lax.rem(y + order[n], 4)
         for b in range(4):
             s = 4 * from_y + b
@@ -246,6 +246,30 @@
             total[...] += part
         else:
             mixed_ref[...] = (total[...] + part).astype(jnp.bfloat16)
+
+    for k in range(3):
+        mix(k)
+
+    @pl.when(has_right)
+    def _():
+        halo(gc, 0, 2).wait_recv()
+
+    @pl.when(jnp.logical_not(has_right))
+    def _():
+        gc[5] = jnp.zeros(gc.shape[1:], gc.dtype)
+
+    back(3)
+    mix(3)
+
+    @pl.when(has_left)
+    def _():
+        halo(gc, 1, 2).wait_recv()
+
+    @pl.when(jnp.logical_not(has_left))
+    def _():
+        gc[0] = jnp.zeros(gc.shape[1:], gc.dtype)
+
+    back(0)
 
     for q in range(4):
         for n in range(4):

time: 40.2 us -> 36.8 us (0.915)
  the two profiles are of different devices: /device:TPU:20 before, /device:TPU:14 now
where the time goes in v2:
time: 36.8 us; the launch traced here: 36.7 us
  Pallas kernels  34.6 us (94%)
  local copies, waits for them, and re-layouts  1.49 us (4%)
  between operations  0.64 us (2%)
    pallas_call x1, Pallas kernels, body(): pl.pallas_call(functools.partial(kernel, n_ctx), out_shape=(jax.ShapeDtyp...  34.6 us
    unnamed x2, local copies, waits for them, and re-layouts  1.49 us

profile of v2, /device:TPU:14, one launch (start us, length us, event | category | flops | bytes accessed | tf_op | source)
XLA Modules:
  0.0 36.7 jit_solution(2805809371222549362)
XLA Ops:
  0.6 34.6 %conv_mix_grad.1 = (bf16[1536,128]{1,0:T(8,128)(2,1)S(1)}, bf16[96,2048]{1,0:T(8,128)(2,1)S(1)}) custom-call(bf16[96,2048]{1,0:T(8,128)(2,1)} %x_hbm.1, bf16[3,96,1536]{2,1,0:T(8,128)(2,1)} %bitcast.1, bf16[1536,1536]{1,0:T(8,128)(2,1)} %pw_hbm.1, bf16[1536,128]{1,0:T(8,128)(2,1)} %cot_hbm.1), custom_call_target="tpu_custom_call" | custom-call | tf_op jit(solution)/shard_map/conv_mix_grad/pallas_call | solution.py:292
  35.2 0.7 %copy.8 = bf16[1536,128]{1,0:T(8,128)(2,1)} copy(bf16[1536,128]{1,0:T(8,128)(2,1)S(1)} %get-tuple-element.4) | data formatting | bytes 786432
  36.0 0.7 %copy.9 = bf16[96,2048]{1,0:T(8,128)(2,1)} copy(bf16[96,2048]{1,0:T(8,128)(2,1)S(1)} %get-tuple-element.5) | data formatting | bytes 786432

commit v3 on v2

--- a/solution.py
+++ b/solution.py
@@ -24,7 +24,7 @@
 
 def kernel(
     n_ctx, x_hbm, wt_hbm, pw_hbm, cot_hbm, mixed_ref, gin_ref,
-    xc, gc, wwin, pw_v, cot_v, cot_t, slope, act_send, act_recv, ga_send, ga_recv, total,
+    xc, gc, wwin, pw_v, cot_v, cot_t, slope, act_send, act_recv, ga_send, ga_recv, total, w_cat, wt_cat,
     load_sem, halo_send, halo_recv, act_ssem, act_rsem, ga_ssem, ga_rsem,
 ):
     width, block = act_send.shape[1:]
@@ -108,36 +108,9 @@
             else:
                 pltpu.make_async_copy(ga_send.at[4 * n + low], ga_recv.at[me], ga_rsem.at[me]).start()
 
-    grad_active(0)
-    for q in range(4):
-        x_loads[q].wait()
-    pl.semaphore_wait(barrier, 15 + has_left.astype(jnp.int32) + has_right.astype(jnp.int32))
-    pl.when(has_right)(lambda: halo(xc, 1, 0).start())
-    pl.when(has_left)(lambda: halo(xc, 0, 0).start())
-    send_ga(0)
-    for n in range(1, 4):
-        grad_active(n)
-        send_ga(n)
-
-    w_load.wait()
-    rows = lax.broadcasted_iota(jnp.int32, (width, 256), 0)
-    lanes = lax.broadcasted_iota(jnp.int32, (width, 256), 1)
-    pick = jnp.where(lanes == rows + off, 1.0, 0.0).astype(jnp.bfloat16)
-    w_cat = lax.dot_general(
-        pick, wwin[...].reshape(TAPS * width, 256), NT, preferred_element_type=jnp.float32
-    ).astype(jnp.bfloat16)
-    depth = lax.broadcasted_iota(jnp.int32, (256, TAPS * width), 0)
-    column = lax.broadcasted_iota(jnp.int32, (256, TAPS * width), 1)
-    wt_cat = jnp.zeros((width, TAPS * width), jnp.float32)
-    for t in range(TAPS):
-        hit = (depth == column - width * t + off) & (column >= width * t) & (column < width * (t + 1))
-        place = jnp.where(hit, 1.0, 0.0).astype(jnp.bfloat16)
-        wt_cat = wt_cat + jnp.dot(wwin[t], place, preferred_element_type=jnp.float32)
-    wt_cat = wt_cat.astype(jnp.bfloat16)
-
     def conv(q):
         signal = jnp.concatenate([xc[q], xc[q + 1], xc[q + 2]], axis=0)
-        act, tilt = gelu_and_slope(jnp.dot(w_cat, signal, preferred_element_type=jnp.float32))
+        act, tilt = gelu_and_slope(jnp.dot(w_cat[...], signal, preferred_element_type=jnp.float32))
         slope[q] = tilt
         act = act.astype(jnp.bfloat16)
         for b in range(4):
@@ -169,10 +142,59 @@
     def wait_sent(q_sems, buffer):
         pltpu.make_async_copy(buffer, buffer, q_sems).wait()
 
-    conv(1)
-    send_act(1)
-    conv(2)
-    send_act(2)
+    def kernel_taps():
+        w_load.wait()
+        rows = lax.broadcasted_iota(jnp.int32, (width, 256), 0)
+        lanes = lax.broadcasted_iota(jnp.int32, (width, 256), 1)
+        pick = jnp.where(lanes == rows + off, 1.0, 0.0).astype(jnp.bfloat16)
+        w = lax.dot_general(
+            pick, wwin[...].reshape(TAPS * width, 256), NT, preferred_element_type=jnp.float32
+        )
+        w_cat[...] = w.astype(jnp.bfloat16)
+        depth = lax.broadcasted_iota(jnp.int32, (256, TAPS * width), 0)
+        column = lax.broadcasted_iota(jnp.int32, (256, TAPS * width), 1)
+        wt = jnp.zeros((width, TAPS * width), jnp.float32)
+        for t in range(TAPS):
+            hit = (depth == column - width * t + off) & (column >= width * t) & (column < width * (t + 1))
+            place = jnp.where(hit, 1.0, 0.0).astype(jnp.bfloat16)
+            wt = wt + jnp.dot(wwin[t], place, preferred_element_type=jnp.float32)
+        wt_cat[...] = wt.astype(jnp.bfloat16)
+
+    early = (lax.rem(me_ctx, n_ctx // 2) == 0) & (me_ctx + me > 0)
+    grad_active(0)
+    for q in range(4):
+        x_loads[q].wait()
+
+    @pl.when(early)
+    def _():
+        for n in range(1, 4):
+            grad_active(n)
+        kernel_taps()
+        conv(1)
+        conv(2)
+
+    pl.semaphore_wait(barrier, 15 + has_left.astype(jnp.int32) + has_right.astype(jnp.int32))
+    pl.when(has_right)(lambda: halo(xc, 1, 0).start())
+    pl.when(has_left)(lambda: halo(xc, 0, 0).start())
+    send_ga(0)
+
+    @pl.when(early)
+    def _():
+        for n in range(1, 4):
+            send_ga(n)
+        send_act(1)
+        send_act(2)
+
+    @pl.when(jnp.logical_not(early))
+    def _():
+        for n in range(1, 4):
+            grad_active(n)
+            send_ga(n)
+        kernel_taps()
+        conv(1)
+        send_act(1)
+        conv(2)
+        send_act(2)
 
     @pl.when(has_left)
     def _():
@@ -220,7 +242,7 @@
     def back(q):
         signal = jnp.concatenate([gc[q + 2], gc[q + 1], gc[q]], axis=0)
         gin_ref[:, pl.ds(STEP * q, STEP)] = jnp.dot(
-            wt_cat, signal, preferred_element_type=jnp.float32
+            wt_cat[...], signal, preferred_element_type=jnp.float32
         ).astype(jnp.bfloat16)
 
     back(1)
@@ -284,12 +306,23 @@
         pl.when(has_right)(lambda: halo(buffer, 1, base).wait_send())
 
 
+def write_out(mixed_ref, gin_ref, mixed_hbm, gin_hbm, sem):
+    copies = (
+        pltpu.make_async_copy(mixed_ref, mixed_hbm, sem.at[0]),
+        pltpu.make_async_copy(gin_ref, gin_hbm, sem.at[1]),
+    )
+    for copy in copies:
+        copy.start()
+    for copy in copies:
+        copy.wait()
+
+
 def body(n_ctx, inputs, conv_weight, pw_weight, cotangent):
     width, length = inputs.shape
     channels, block = cotangent.shape
     bf16, f32 = jnp.bfloat16, jnp.float32
     dma = pltpu.SemaphoreType.DMA
-    return pl.pallas_call(
+    mixed, grad_inputs = pl.pallas_call(
         functools.partial(kernel, n_ctx),
         out_shape=(
             jax.ShapeDtypeStruct((channels, block), bf16),
@@ -310,6 +343,8 @@
             pltpu.VMEM((16, width, block), bf16),
             pltpu.VMEM((16, width, block), bf16),
             pltpu.VMEM((channels, block), f32),
+            pltpu.VMEM((width, TAPS * width), bf16),
+            pltpu.VMEM((width, TAPS * width), bf16),
             dma((10,)),
             dma((4,)),
             dma((4,)),
@@ -326,6 +361,18 @@
         pltpu.with_memory_space_constraint(a, pltpu.HBM)
         for a in (inputs, jnp.transpose(conv_weight, (0, 2, 1)), pw_weight, cotangent)
     ))
+    return pl.pallas_call(
+        write_out,
+        out_shape=(
+            jax.ShapeDtypeStruct(mixed.shape, bf16),
+            jax.ShapeDtypeStruct(grad_inputs.shape, bf16),
+        ),
+        in_specs=[pl.BlockSpec(memory_space=pl.ANY)] * 2,
+        out_specs=[pl.BlockSpec(memory_space=pltpu.HBM)] * 2,
+        scratch_shapes=[dma((2,))],
+        compiler_params=pltpu.CompilerParams(vmem_limit_bytes=4 * 1024 * 1024),
+        name="write_out",
+    )(mixed, grad_inputs)
 
 
 def solution(mesh):

time: 36.8 us -> 36.2 us (0.984)
  local copies, waits for them, and re-layouts: 1.49 us -> 0 us
  Pallas kernels: 34.6 us -> 35.5 us
    unnamed x2 -> x0, local copies, waits for them, and re-layouts: 1.49 us -> none
    pallas_call x0 -> x1, Pallas kernels: none -> 0.89 us  [body(): pl.pallas_call(write_out, out_shape=(jax.ShapeDtypeStruct(mixed.shape, bf...]
where the time goes in v3:
time: 36.2 us; the launch traced here: 36.1 us
  Pallas kernels  35.5 us (98%)
  between operations  0.64 us (2%)
    pallas_call x1, Pallas kernels, body(): pl.pallas_call(functools.partial(kernel, n_ctx), out_shape=(jax.ShapeDtyp...  34.6 us
    pallas_call x1, Pallas kernels, body(): pl.pallas_call(write_out, out_shape=(jax.ShapeDtypeStruct(mixed.shape, bf...  0.89 us

profile of v3, /device:TPU:14, one launch (start us, length us, event | category | flops | bytes accessed | tf_op | source)
XLA Modules:
  0.0 36.1 jit_solution(3811256667802522000)
XLA Ops:
  0.6 34.6 %conv_mix_grad.1 = (bf16[1536,128]{1,0:T(8,128)(2,1)S(1)}, bf16[96,2048]{1,0:T(8,128)(2,1)S(1)}) custom-call(bf16[96,2048]{1,0:T(8,128)(2,1)} %x_hbm.1, bf16[3,96,1536]{2,1,0:T(8,128)(2,1)} %bitcast.1, bf16[1536,1536]{1,0:T(8,128)(2,1)} %pw_hbm.1, bf16[1536,128]{1,0:T(8,128)(2,1)} %cot_hbm.1), custom_call_target="tpu_custom_call" | custom-call | tf_op jit(solution)/shard_map/conv_mix_grad/pallas_call | solution.py:325
  35.2 0.9 %write_out.1 = (bf16[1536,128]{1,0:T(8,128)(2,1)}, bf16[96,2048]{1,0:T(8,128)(2,1)}) custom-call(bf16[1536,128]{1,0:T(8,128)(2,1)S(1)} %get-tuple-element.4.mixed_ref, bf16[96,2048]{1,0:T(8,128)(2,1)S(1)} %get-tuple-element.5.gin_ref), custom_call_target="tpu_custom_call" | custom-call | tf_op jit(solution)/shard_map/write_out/pallas_call | solution.py:364

commit v4 on v3

--- a/solution.py
+++ b/solution.py
@@ -49,7 +49,7 @@
 
     cot_load = pltpu.make_async_copy(cot_hbm, cot_v, load_sem.at[5])
     cot_load.start()
-    order = (1, 3, 2, 0)
+    order = (2, 1, 3, 0)
     pw_loads = []
 
     def load_pw(n):
@@ -192,9 +192,9 @@
             send_ga(n)
         kernel_taps()
         conv(1)
-        send_act(1)
+        pl.when(me_ctx != seam)(lambda: send_act(1))
         conv(2)
-        send_act(2)
+        pl.when(me_ctx != seam)(lambda: send_act(2))
 
     @pl.when(has_left)
     def _():
@@ -233,8 +233,8 @@
 
     @pl.when(me_ctx == seam)
     def _():
-        send_act(0)
-        send_act(3)
+        for q in range(4):
+            send_act(q)
 
     grad_conv(1)
     grad_conv(2)
@@ -248,7 +248,7 @@
     back(1)
     back(2)
 
-    visit = (3, 0, 1, 2)
+    visit = (3, 1, 2, 0)
 
     def mix(k):
         n = visit[k]

time: 36.2 us -> 35 us (0.967)
  the two profiles are of different devices: /device:TPU:14 before, /device:TPU:30 now
where the time goes in v4:
time: 35 us; the launch traced here: 34.9 us
  Pallas kernels  34.2 us (98%)
  between operations  0.64 us (2%)
    pallas_call x1, Pallas kernels, body(): pl.pallas_call(functools.partial(kernel, n_ctx), out_shape=(jax.ShapeDtyp...  33.4 us
    pallas_call x1, Pallas kernels, body(): pl.pallas_call(write_out, out_shape=(jax.ShapeDtypeStruct(mixed.shape, bf...  0.89 us

profile of v4, /device:TPU:30, one launch (start us, length us, event | category | flops | bytes accessed | tf_op | source)
XLA Modules:
  0.0 34.9 jit_solution(6535113571417498523)
XLA Ops:
  0.6 33.4 %conv_mix_grad.1 = (bf16[1536,128]{1,0:T(8,128)(2,1)S(1)}, bf16[96,2048]{1,0:T(8,128)(2,1)S(1)}) custom-call(bf16[96,2048]{1,0:T(8,128)(2,1)} %x_hbm.1, bf16[3,96,1536]{2,1,0:T(8,128)(2,1)} %bitcast.1, bf16[1536,1536]{1,0:T(8,128)(2,1)} %pw_hbm.1, bf16[1536,128]{1,0:T(8,128)(2,1)} %cot_hbm.1), custom_call_target="tpu_custom_call" | custom-call | tf_op jit(solution)/shard_map/conv_mix_grad/pallas_call | solution.py:325
  34.0 0.9 %write_out.1 = (bf16[1536,128]{1,0:T(8,128)(2,1)}, bf16[96,2048]{1,0:T(8,128)(2,1)}) custom-call(bf16[1536,128]{1,0:T(8,128)(2,1)S(1)} %get-tuple-element.4.mixed_ref, bf16[96,2048]{1,0:T(8,128)(2,1)S(1)} %get-tuple-element.5.gin_ref), custom_call_target="tpu_custom_call" | custom-call | tf_op jit(solution)/shard_map/write_out/pallas_call | solution.py:364
